TPU v7x, 32 devices: a whole 2x2x4 slice. The times are simulated.
32 devices in a mesh: dp: 8 (over z, x), mp: 4 (over y, core).
Axes of the slice: x: 2, y: 2, z: 4, core: 2. Of those that a mesh axis runs over, the one named last changes fastest.
Arguments:
- block_in: bfloat16 [16384, 1024], P('dp', 'mp')
- out_grad: bfloat16 [16384, 1024], P('dp', 'mp')
- lengths: int32 [16], P('dp'), may hold values from 256 to 1024
- group_ids: int32 [16], P('dp'), may hold values from 0 to 7
- time_embed: float32 [8, 1024], replicated, may hold values from -6 to 6
- weights: float32 [1024, 14, 1024], P('dp', None, 'mp')
- first_moments: float32 [1024, 14, 1024], P('dp', None, 'mp')
- second_moments: float32 [1024, 14, 1024], P('dp', None, 'mp'), as said below
- owners: int32 [14, 8], replicated, may hold values from 0 to 7, each once within a row
- left_basis: float32 [14, 1024, 128], P(None, 'dp'), may hold values from -1 to 1, as said below
- right_basis: float32 [14, 1024, 256], P(None, 'mp'), may hold values from -1 to 1, as said below
- biases: float32 [13, 1024], P(None, 'mp'), may hold values from -2.5 to 2.5
- bias_first: float32 [13, 1024], P(None, 'mp')
- bias_second: float32 [13, 1024], P(None, 'mp'), as said below
Outputs:
- block_out: bfloat16 [16384, 1024], P('dp', 'mp')
- input_grad: float32 [16384, 1024], P('dp', 'mp')
- weight_grads: float32 [1024, 14, 1024], P('dp', None, 'mp')
- new_first: float32 [1024, 14, 1024], P('dp', None, 'mp')
- new_second: float32 [1024, 14, 1024], P('dp', None, 'mp')
- new_weights: float32 [1024, 14, 1024], P('dp', None, 'mp')
- new_weights_low: bfloat16 [1024, 14, 1024], P('dp', None, 'mp')
- new_bias_first: float32 [13, 1024], P(None, 'mp')
- new_bias_second: float32 [13, 1024], P(None, 'mp')
- new_biases: float32 [13, 1024], P(None, 'mp')
Inputs may be any that keep to these rules, and one draw needn't show every extreme that they name: Each block left_basis[k, a * 128 to a * 128 + 127, :] is an orthogonal matrix. Each block right_basis[k, c * 256 to c * 256 + 255, :] is an orthogonal matrix. `second_moments`: positive. `bias_second`: positive.
All inputs are finite; a program needn't handle non-finite values.
Results may differ from a plain program's by a relative error of at most 0.02.
The roundings to bfloat16 on the way count: a program that leaves them out, or rounds other values in their place, can miss the bound.
Values may be sent and summed in bfloat16 or wider, within the bound.
No kernel may reach another device: no remote copies, remote signals or barrier semaphores. Data moves between devices by JAX's collectives and lax.ppermute only.
A program may use at most 192 MiB of HBM per device.

v0:
```python
import jax
import jax.numpy as jnp
from jax import lax
from jax.sharding import PartitionSpec as P

D = 1024
HEAD_DIM = 64
LEN = 1024
UTT_DEV = 2
GROUPS = 8
STEP = 10
norm_epsilon = 1e-06
soap_first = 0.95
soap_second = 0.95
soap_epsilon = 1e-08
soap_rate = 0.05
soap_decay = 0.01
vector_first = 0.9
vector_second = 0.999
vector_epsilon = 1e-08
vector_rate = 0.1
masked_score = -1e30


def true_order(gathered, owners):
    block_count = owners.shape[1]
    blocks = gathered.reshape(
        block_count, gathered.shape[0] // block_count, gathered.shape[1], gathered.shape[2]
    )
    picked = [
        jnp.take(blocks[:, :, slot_index, :], owners[slot_index], axis=0)
        for slot_index in range(owners.shape[0])
    ]
    return jnp.stack(picked, axis=2).reshape(gathered.shape)


def stored_order(values, owners):
    block_count = owners.shape[1]
    blocks = values.reshape(
        block_count, values.shape[0] // block_count, values.shape[1], values.shape[2]
    )
    placed = [
        jnp.take(blocks[:, :, slot_index, :], jnp.argsort(owners[slot_index]), axis=0)
        for slot_index in range(owners.shape[0])
    ]
    return jnp.stack(placed, axis=2).reshape(values.shape)


def gather_block(low_weights, owners):
    whole_rows = lax.all_gather(low_weights[:, :8, :], "dp", axis=0, tiled=True)
    return true_order(whole_rows, owners[:8])


def reduce_grads(values):
    return lax.psum_scatter(
        values.astype(jnp.bfloat16), "dp", scatter_dimension=0, tiled=True
    ).astype(jnp.float32)


def branch_total(partial_rows):
    return lax.psum_scatter(
        partial_rows.astype(jnp.bfloat16), "mp", scatter_dimension=1, tiled=True
    ).astype(jnp.float32)


def branch_spread(grad_rows):
    return lax.all_gather(grad_rows, "mp", axis=1, tiled=True)


def gelu_tanh(values):
    return jax.nn.gelu(values, approximate=True)


def rotary_tables():
    half_dim = HEAD_DIM // 2
    places = jnp.arange(LEN, dtype=jnp.float32)
    frequencies = 10000.0 ** (-(jnp.arange(half_dim, dtype=jnp.float32) * 2.0 / HEAD_DIM))
    angles = places[:, None] * frequencies[None, :]
    return (jnp.cos(angles)[:, None, :], jnp.sin(angles)[:, None, :])


def rotate(values, cosine_table, sine_table, direction_sign):
    pair_view = values.reshape(values.shape[0], values.shape[1], values.shape[2] // 2, 2)
    even_part = pair_view[..., 0]
    odd_part = pair_view[..., 1]
    turned = jnp.stack(
        [
            even_part * cosine_table - direction_sign * odd_part * sine_table,
            odd_part * cosine_table + direction_sign * even_part * sine_table,
        ],
        axis=-1,
    )
    return turned.reshape(values.shape)


def modulated(values, shift_row, scale_row):
    totals = lax.psum((jnp.sum(values, axis=1), jnp.sum(values * values, axis=1)), "mp")
    row_mean = totals[0] / D
    spread = totals[1] / D - row_mean * row_mean
    inverse = lax.rsqrt(spread + norm_epsilon)
    normed = (values - row_mean[:, None]) * inverse[:, None]
    low_rows = (normed * (1.0 + scale_row) + shift_row).astype(jnp.bfloat16)
    return (lax.all_gather(low_rows, "mp", axis=1, tiled=True), normed, inverse)


def norm_back(partial_rows, normed, inverse, scale_row):
    grad_hidden = lax.psum_scatter(
        partial_rows.astype(jnp.bfloat16), "mp", scatter_dimension=1, tiled=True
    ).astype(jnp.float32)
    grad_normed = grad_hidden * (1.0 + scale_row)
    totals = lax.psum((jnp.sum(grad_normed, axis=1), jnp.sum(grad_normed * normed, axis=1)), "mp")
    grad_rows = inverse[:, None] * (
        grad_normed - totals[0][:, None] / D - normed * totals[1][:, None] / D
    )
    return (grad_rows, jnp.sum(grad_hidden, axis=0), jnp.sum(grad_hidden * normed, axis=0))


def attend(queries, keys_in, values_in, valid_rows):
    score_scale = HEAD_DIM ** (-0.5)
    block_rows = LEN // 2
    outputs = []
    totals = []
    for offset in range(0, LEN, block_rows):
        scores = (
            jnp.einsum(
                "qhd,khd->hqk",
                queries[offset : offset + block_rows],
                keys_in,
                preferred_element_type=jnp.float32,
            )
            * score_scale
        )
        scores = jnp.where(valid_rows[None, None, :], scores, masked_score)
        row_top = jnp.max(scores, axis=2, keepdims=True)
        row_total = row_top + jnp.log(jnp.sum(jnp.exp(scores - row_top), axis=2, keepdims=True))
        chances = jnp.exp(scores - row_total).astype(jnp.bfloat16)
        outputs.append(
            jnp.einsum("hqk,khd->qhd", chances, values_in, preferred_element_type=jnp.float32)
        )
        totals.append(row_total)
    return (jnp.concatenate(outputs, axis=0).astype(jnp.bfloat16), totals)


def attend_back(queries, keys_in, values_in, valid_rows, totals, grad_mixed):
    score_scale = HEAD_DIM ** (-0.5)
    block_rows = LEN // 2
    grad_keys = jnp.zeros(keys_in.shape, jnp.float32)
    grad_values = jnp.zeros(values_in.shape, jnp.float32)
    grad_queries = []
    for position, offset in enumerate(range(0, LEN, block_rows)):
        query_rows = queries[offset : offset + block_rows]
        grad_rows = grad_mixed[offset : offset + block_rows]
        scores = (
            jnp.einsum("qhd,khd->hqk", query_rows, keys_in, preferred_element_type=jnp.float32)
            * score_scale
        )
        scores = jnp.where(valid_rows[None, None, :], scores, masked_score)
        soft_chances = jnp.exp(scores - totals[position])
        grad_values = grad_values + jnp.einsum(
            "hqk,qhd->khd",
            soft_chances.astype(jnp.bfloat16),
            grad_rows,
            preferred_element_type=jnp.float32,
        )
        grad_chances = jnp.einsum(
            "qhd,khd->hqk", grad_rows, values_in, preferred_element_type=jnp.float32
        )
        inner = jnp.sum(soft_chances * grad_chances, axis=2, keepdims=True)
        grad_scores = (soft_chances * (grad_chances - inner)).astype(jnp.bfloat16)
        grad_queries.append(
            jnp.einsum("hqk,khd->qhd", grad_scores, keys_in, preferred_element_type=jnp.float32)
            * score_scale
        )
        grad_keys = (
            grad_keys
            + jnp.einsum(
                "hqk,qhd->khd", grad_scores, query_rows, preferred_element_type=jnp.float32
            )
            * score_scale
        )
    return (jnp.concatenate(grad_queries, axis=0), grad_keys, grad_values)


def body(
    block_in,
    out_grad,
    lengths,
    group_ids,
    time_embed,
    weights,
    first_moments,
    second_moments,
    owners,
    left_basis,
    right_basis,
    biases,
    bias_first,
    bias_second,
):
    highest = lax.Precision.HIGHEST
    shard_width = weights.shape[2]
    head_count = shard_width // HEAD_DIM
    group_hits = (group_ids[:, None] == jnp.arange(GROUPS, dtype=jnp.int32)[None, :]).astype(
        jnp.float32
    )
    embedded = jnp.dot(group_hits, time_embed, precision=highest)
    condition = jax.nn.silu(embedded).astype(jnp.bfloat16)
    low_weights = weights.astype(jnp.bfloat16)
    mod_whole = lax.all_gather(low_weights[:, 8:, :], "dp", axis=0, tiled=True)
    mod_true = true_order(mod_whole, owners[8:])
    modulation = (
        jnp.einsum("ud,dkc->ukc", condition, mod_true, preferred_element_type=jnp.float32)
        + biases[7:]
    )
    cosine_table, sine_table = rotary_tables()
    outputs = []
    input_rows = []
    mod_grads = []
    weight_total = jnp.zeros((D, 8, shard_width), jnp.float32)
    bias_total = jnp.zeros((7, shard_width), jnp.float32)
    for utterance in range(UTT_DEV):
        block_now = gather_block(low_weights, owners)
        mod_row = modulation[utterance]
        rows_x = block_in[utterance * LEN : (utterance + 1) * LEN].astype(jnp.float32)
        cotangent = out_grad[utterance * LEN : (utterance + 1) * LEN].astype(jnp.float32)
        valid_rows = jnp.arange(LEN, dtype=jnp.int32) < lengths[utterance]
        keep_rows = valid_rows.astype(jnp.float32)[:, None]
        normed_in, first_norm, first_inverse = modulated(rows_x, mod_row[0], mod_row[1])
        projected = (
            jnp.einsum(
                "td,dkc->tkc", normed_in, block_now[:, 0:3, :], preferred_element_type=jnp.float32
            )
            + biases[0:3]
        )
        queries = rotate(
            projected[:, 0, :].reshape(LEN, head_count, HEAD_DIM), cosine_table, sine_table, 1.0
        ).astype(jnp.bfloat16)
        keys_in = rotate(
            projected[:, 1, :].reshape(LEN, head_count, HEAD_DIM), cosine_table, sine_table, 1.0
        ).astype(jnp.bfloat16)
        values_in = projected[:, 2, :].reshape(LEN, head_count, HEAD_DIM).astype(jnp.bfloat16)
        mixed, totals = attend(queries, keys_in, values_in, valid_rows)
        mixed_rows = mixed.reshape(LEN, shard_width)
        attended = (
            branch_total(
                jnp.einsum(
                    "tc,oc->to", mixed_rows, block_now[:, 3, :], preferred_element_type=jnp.float32
                )
            )
            + biases[3]
        ) * keep_rows
        middle = rows_x + mod_row[2] * attended
        normed_mid, second_norm, second_inverse = modulated(middle, mod_row[3], mod_row[4])
        hidden = (
            jnp.einsum(
                "td,dec->tec", normed_mid, block_now[:, 4:6, :], preferred_element_type=jnp.float32
            )
            + biases[4:6]
        )
        active = gelu_tanh(hidden).astype(jnp.bfloat16)
        fed_rows = (
            branch_total(
                jnp.einsum(
                    "tec,oec->to", active, block_now[:, 6:8, :], preferred_element_type=jnp.float32
                )
            )
            + biases[6]
        )
        outputs.append((middle + mod_row[5] * fed_rows).astype(jnp.bfloat16))
        grad_fed = (mod_row[5] * cotangent).astype(jnp.bfloat16)
        grad_fed_whole = branch_spread(grad_fed)
        grad_out_weight = jnp.einsum(
            "to,tec->oec", grad_fed_whole, active, preferred_element_type=jnp.float32
        )
        grad_active = jnp.einsum(
            "to,oec->tec", grad_fed_whole, block_now[:, 6:8, :], preferred_element_type=jnp.float32
        )
        grad_hidden = jax.vjp(gelu_tanh, hidden)[1](grad_active)[0].astype(jnp.bfloat16)
        grad_in_weight = jnp.einsum(
            "td,tec->dec", normed_mid, grad_hidden, preferred_element_type=jnp.float32
        )
        grad_mid_norm, shift_two, scale_two = norm_back(
            jnp.einsum(
                "tec,dec->td", grad_hidden, block_now[:, 4:6, :], preferred_element_type=jnp.float32
            ),
            second_norm,
            second_inverse,
            mod_row[4],
        )
        grad_middle = cotangent + grad_mid_norm
        grad_attended = (mod_row[2] * grad_middle * keep_rows).astype(jnp.bfloat16)
        grad_attended_whole = branch_spread(grad_attended)
        grad_proj_weight = jnp.einsum(
            "to,tc->oc", grad_attended_whole, mixed_rows, preferred_element_type=jnp.float32
        )
        grad_mixed = jnp.einsum(
            "to,oc->tc", grad_attended_whole, block_now[:, 3, :], preferred_element_type=jnp.float32
        ).astype(jnp.bfloat16)
        grad_query_turned, grad_key_turned, grad_values = attend_back(
            queries,
            keys_in,
            values_in,
            valid_rows,
            totals,
            grad_mixed.reshape(LEN, head_count, HEAD_DIM),
        )
        grad_projected = jnp.stack(
            [
                rotate(grad_query_turned, cosine_table, sine_table, -1.0).reshape(LEN, shard_width),
                rotate(grad_key_turned, cosine_table, sine_table, -1.0).reshape(LEN, shard_width),
                grad_values.reshape(LEN, shard_width),
            ],
            axis=1,
        ).astype(jnp.bfloat16)
        grad_qkv_weight = jnp.einsum(
            "td,tkc->dkc", normed_in, grad_projected, preferred_element_type=jnp.float32
        )
        grad_in_norm, shift_one, scale_one = norm_back(
            jnp.einsum(
                "tkc,dkc->td",
                grad_projected,
                block_now[:, 0:3, :],
                preferred_element_type=jnp.float32,
            ),
            first_norm,
            first_inverse,
            mod_row[1],
        )
        input_rows.append(grad_middle + grad_in_norm)
        mod_grads.append(
            jnp.stack(
                [
                    shift_one,
                    scale_one,
                    jnp.sum(grad_middle * attended, axis=0),
                    shift_two,
                    scale_two,
                    jnp.sum(cotangent * fed_rows, axis=0),
                ]
            )
        )
        weight_total = weight_total + jnp.concatenate(
            [grad_qkv_weight, grad_proj_weight[:, None, :], grad_in_weight, grad_out_weight], axis=1
        )
        bias_total = bias_total + jnp.concatenate(
            [
                jnp.sum(grad_projected.astype(jnp.float32), axis=0),
                jnp.sum(grad_attended.astype(jnp.float32), axis=0)[None, :],
                jnp.sum(grad_hidden.astype(jnp.float32), axis=0),
                jnp.sum(grad_fed.astype(jnp.float32), axis=0)[None, :],
            ],
            axis=0,
        )
    grad_mods = jnp.stack(mod_grads)
    grad_mod_weight = jnp.einsum(
        "ud,ukc->dkc", condition.astype(jnp.float32), grad_mods, precision=highest
    )
    reduced = reduce_grads(
        stored_order(jnp.concatenate([weight_total, grad_mod_weight], axis=1), owners)
    )
    bias_local = jnp.concatenate([bias_total, jnp.sum(grad_mods, axis=0)], axis=0)
    bias_grad = lax.psum(bias_local, "dp")
    turned = jnp.einsum("kij,ikc->jkc", left_basis, reduced, precision=highest)
    turned = jnp.einsum("jkc,kce->jke", turned, right_basis, precision=highest)
    first_new = soap_first * first_moments + (1.0 - soap_first) * turned
    second_new = soap_second * second_moments + (1.0 - soap_second) * turned * turned
    direction = (
        first_new
        / (1.0 - soap_first**STEP)
        / (jnp.sqrt(second_new / (1.0 - soap_second**STEP)) + soap_epsilon)
    )
    rotated_back = jnp.einsum("kij,jke->ike", left_basis, direction, precision=highest)
    rotated_back = jnp.einsum("ike,kce->ikc", rotated_back, right_basis, precision=highest)
    new_weights = weights - soap_rate * (rotated_back + soap_decay * weights)
    bias_first_new = vector_first * bias_first + (1.0 - vector_first) * bias_grad
    bias_second_new = vector_second * bias_second + (1.0 - vector_second) * bias_grad * bias_grad
    new_biases = biases - vector_rate * (bias_first_new / (1.0 - vector_first**STEP)) / (
        jnp.sqrt(bias_second_new / (1.0 - vector_second**STEP)) + vector_epsilon
    )
    return (
        jnp.concatenate(outputs, axis=0),
        jnp.concatenate(input_rows, axis=0),
        reduced,
        first_new,
        second_new,
        new_weights,
        new_weights.astype(jnp.bfloat16),
        bias_first_new,
        bias_second_new,
        new_biases,
    )


def solution(mesh):
    return jax.shard_map(
        body,
        mesh=mesh,
        in_specs=(
            P("dp", "mp"),
            P("dp", "mp"),
            P("dp"),
            P("dp"),
            P(),
            P("dp", None, "mp"),
            P("dp", None, "mp"),
            P("dp", None, "mp"),
            P(),
            P(None, "dp", None),
            P(None, "mp", None),
            P(None, "mp"),
            P(None, "mp"),
            P(None, "mp"),
        ),
        out_specs=(
            P("dp", "mp"),
            P("dp", "mp"),
            P("dp", None, "mp"),
            P("dp", None, "mp"),
            P("dp", None, "mp"),
            P("dp", None, "mp"),
            P("dp", None, "mp"),
            P(None, "mp"),
            P(None, "mp"),
            P(None, "mp"),
        ),
        check_vma=False,
    )
```

profile of v0, /device:TPU:0, one launch (start us, length us, event | category | flops | bytes accessed | tf_op | source)
XLA Modules:
  0.0 1064.8 jit_solution(13720281788594007767)
XLA Ops:
  13.4 12.6 %all-reduce.3 = (f32[1024]{0:T(1024)S(1)}, f32[1024]{0:T(1024)S(1)}, f32[1024]{0:T(1024)S(1)}, f32[1024]{0:T(1024)S(1)}) all-reduce(f32[1024]{0:T(1024)S(1)} %get-tuple-element.61, f32[1024]{0:T(1024)S(1)} %get-tuple-element.60, f32[1024]{0:T(1024)S(1)} %get-tuple-element.62, ...), channel_id=1, replica_groups=mesh['dp'=8,'mp'=4] {'mp'}, use_global_device_ids=true, to_apply=%region_3.5 | all-reduce | flops 4096 | bytes 32768 | tf_op jit(solution)/shard_map/psum | solution.py:97
  26.9 47.2 %all-gather.11.cloned.1.call-done = bf16[1024,6,256]{2,0,1:T(8,128)(2,1)} async-done(((bf16[128,6,256]{2,0,1:T(8,128)(2,1)}), bf16[1024,6,256]{2,0,1:T(8,128)(2,1)}) %all-gather.11.cloned.1.call-update) | async-done | bytes 3145744 | tf_op jit(solution)/shard_map/all_gather | solution.py:209
  74.1 3.2 slice_bitcast_fusion.22
  99.7 48.6 %all-gather.15.cloned.1.call-done = bf16[1024,8,256]{2,0,1:T(8,128)(2,1)} async-done(((bf16[128,8,256]{2,0,1:T(8,128)(2,1)}), bf16[1024,8,256]{2,0,1:T(8,128)(2,1)}) %all-gather.15.cloned.1.call-update) | async-done | bytes 4194320 | tf_op jit(solution)/shard_map/all_gather | solution.py:50
  148.3 3.8 slice_bitcast_fusion.17
  171.6 3.8 fusion.59
  177.0 19.5 %all-gather.19.cloned.1.call-done = bf16[1024,1024]{1,0:T(8,128)(2,1)} async-done(((bf16[1024,256]{1,0:T(8,128)(2,1)}), bf16[1024,1024]{1,0:T(8,128)(2,1)}) %all-gather.19.cloned.1.call-update) | async-done | bytes 2097168 | tf_op jit(solution)/shard_map/all_gather | solution.py:103
  196.5 3.7 fusion.62
  213.7 8.6 subtract_convert_fusion.4
  225.5 3.4 fusion.131
  233.2 3.4 exponential_reduce_fusion.1
  247.3 2.9 pad_maximum_fusion.10
  251.5 3.5 fusion.132
  259.4 3.4 exponential_reduce_fusion.3
  274.8 4.0 reduce-scatter.14.cloned.1.call-done
  278.8 34.6 %reduce-scatter.10.cloned.1.call-done = bf16[1024,256]{1,0:T(8,128)(2,1)} async-done(((bf16[1024,1024]{1,0:T(8,128)(2,1)}), bf16[1024,256]{1,0:T(8,128)(2,1)}) %reduce-scatter.10.cloned.1.call-update) | async-done | bytes 524304 | tf_op jit(solution)/shard_map/reduce_scatter | solution.py:61
  315.6 10.1 all-reduce.2
  325.8 3.0 add_convert_fusion.3
  328.9 3.1 convert_reduce_fusion.10
  346.2 6.7 all-gather.21.cloned.1.call-done
  352.8 4.5 fusion.32
  357.3 20.5 %all-gather.27.cloned.1.call-done = bf16[1024,1024]{1,0:T(8,128)(2,1)} async-done(((bf16[1024,256]{1,0:T(8,128)(2,1)}), bf16[1024,1024]{1,0:T(8,128)(2,1)}) %all-gather.27.cloned.1.call-update) | async-done | bytes 2097168 | tf_op jit(solution)/shard_map/all_gather | solution.py:67
  377.8 5.4 convert_reduce_fusion.2
  386.9 16.0 %all-gather.17.cloned.1.call-done = bf16[1024,1024]{1,0:T(8,128)(2,1)} async-done(((bf16[1024,256]{1,0:T(8,128)(2,1)}), bf16[1024,1024]{1,0:T(8,128)(2,1)}) %all-gather.17.cloned.1.call-update) | async-done | bytes 2097168 | tf_op jit(solution)/shard_map/all_gather | solution.py:103
  402.8 4.4 fusion.40
  407.2 19.9 %all-gather.23.cloned.1.call-done = bf16[1024,1024]{1,0:T(8,128)(2,1)} async-done(((bf16[1024,256]{1,0:T(8,128)(2,1)}), bf16[1024,1024]{1,0:T(8,128)(2,1)}) %all-gather.23.cloned.1.call-update) | async-done | bytes 2097168 | tf_op jit(solution)/shard_map/all_gather | solution.py:67
  427.1 5.4 convert_reduce_fusion.3
  436.4 4.7 bitcast_convert_fusion.4
  441.2 4.8 bitcast_convert_fusion.5
  461.1 34.0 %reduce-scatter.18.cloned.1.call-done = bf16[1024,256]{1,0:T(8,128)(2,1)} async-done(((bf16[1024,1024]{1,0:T(8,128)(2,1)}), bf16[1024,256]{1,0:T(8,128)(2,1)}) %reduce-scatter.18.cloned.1.call-update) | async-done | bytes 524304 | tf_op jit(solution)/shard_map/reduce_scatter | solution.py:107
  498.0 10.1 all-reduce.1
  508.1 21.0 %reduce-scatter.16.cloned.1.call-done = bf16[1024,256]{1,0:T(8,128)(2,1)} async-done(((bf16[1024,1024]{1,0:T(8,128)(2,1)}), bf16[1024,256]{1,0:T(8,128)(2,1)}) %reduce-scatter.16.cloned.1.call-update) | async-done | bytes 524304 | tf_op jit(solution)/shard_map/reduce_scatter | solution.py:61
  529.2 34.0 %reduce-scatter.12.cloned.1.call-done = bf16[1024,256]{1,0:T(8,128)(2,1)} async-done(((bf16[1024,1024]{1,0:T(8,128)(2,1)}), bf16[1024,256]{1,0:T(8,128)(2,1)}) %reduce-scatter.12.cloned.1.call-update) | async-done | bytes 524304 | tf_op jit(solution)/shard_map/reduce_scatter | solution.py:61
  563.1 4.2 convert_reduce_fusion.11
  569.8 3.9 convert_reduce_fusion.13
  573.8 16.6 %all-gather.29.cloned.1.call-done = bf16[1024,1024]{1,0:T(8,128)(2,1)} async-done(((bf16[1024,256]{1,0:T(8,128)(2,1)}), bf16[1024,1024]{1,0:T(8,128)(2,1)}) %all-gather.29.cloned.1.call-update) | async-done | bytes 2097168 | tf_op jit(solution)/shard_map/all_gather | solution.py:67
  593.6 4.5 fusion.199
  598.1 14.9 %multiply_reduce_fusion = (f32[4,512]{1,0:T(4,128)S(1)}, f32[4,512]{1,0:T(4,128)S(1)}, f32[4,512,1024]{2,1,0:T(8,128)}) fusion(f32[4,512,1024]{2,1,0:T(8,128)} %copy-done.3, f32[4,512]{1,0:T(4,128)S(1)} %log_add_fusion, pred[1024]{0:T(1024)(128)(4,1)S(1)} %iota_compare_fusion, f32[4,512,1024]{2,1,0:T(8,128)} %fusion.199, f32[4,512]{1,0:T(4,128)S(1)} %log_add_fusion.1, ...), kind=kOutput, calls=%fused_computation.31 | convolution fusion | flops 289402880 | bytes 34374656 | tf_op jit(solution)/shard_map/qhd,khd->hqk/dot_general | solution.py:165
  615.2 9.9 multiply_convert_fusion
  635.2 4.5 fusion.197
  639.8 14.1 %multiply_reduce_fusion.2 = (f32[4,512]{1,0:T(4,128)S(1)}, f32[4,512]{1,0:T(4,128)S(1)}, f32[4,512,1024]{2,1,0:T(8,128)}) fusion(f32[4,512,1024]{2,1,0:T(8,128)} %copy-done.2, f32[4,512]{1,0:T(4,128)S(1)} %log_add_fusion.2, pred[1024]{0:T(1024)(128)(4,1)S(1)} %iota_compare_fusion.1, f32[4,512,1024]{2,1,0:T(8,128)} %fusion.197, ...), kind=kOutput, calls=%fused_computation.35 | convolution fusion | flops 289402880 | bytes 34374656 | tf_op jit(solution)/shard_map/qhd,khd->hqk/dot_general | solution.py:165
  656.1 10.3 multiply_convert_fusion.2
  670.5 6.1 fusion.88
  678.7 4.5 fusion.92
  693.1 4.5 fusion.90
  707.3 8.5 subtract_convert_fusion.3
  721.8 3.1 pad_maximum_fusion.17
  729.0 4.9 bitcast_convert_fusion
  734.2 5.4 fusion.142
  739.6 6.6 fusion.87
  748.2 3.1 pad_maximum_fusion.14
  755.4 2.9 pad_maximum_fusion.15
  761.6 5.0 bitcast_convert_fusion.2
  767.0 4.6 fusion.30
  788.7 8.9 maximum_add_fusion
  802.2 10.1 all-reduce
  812.4 3.2 multiply_reduce_fusion.5
  815.7 4.2 fusion.146
  820.0 6.7 pad_maximum_fusion
  826.7 5.7 slice_bitcast_fusion
  911.5 39.7 %psum.135 = f32[13,256]{1,0:T(8,128)S(1)} all-reduce(f32[13,256]{1,0:T(8,128)S(1)} %pad_maximum_fusion.24), channel_id=1, replica_groups=mesh['dp'=8,'mp'=4] {'dp'}, use_global_device_ids=true, to_apply=%region_87.90 | all-reduce | flops 3328 | bytes 26624 | tf_op jit(solution)/shard_map/psum | solution.py:362
  956.6 85.2 %reduce-scatter.26.cloned.1.call-done = bf16[128,14,256]{2,0,1:T(8,128)(2,1)} async-done(((bf16[1024,14,256]{2,0,1:T(8,128)(2,1)}), bf16[128,14,256]{2,0,1:T(8,128)(2,1)}) %reduce-scatter.26.cloned.1.call-update) | async-done | bytes 917520 | tf_op jit(solution)/shard_map/reduce_scatter | solution.py:55
  1044.1 4.3 fusion.46
  1051.3 5.4 fusion.196
  (644 shorter events, 318.9 us)
Async XLA Ops:
  7.2 1034.7 %copy-start = (f32[14,128,128]{2,1,0:T(8,128)S(1)}, f32[14,128,128]{2,1,0:T(8,128)}, u32[]{:S(2)}) copy-start(f32[14,128,128]{2,1,0:T(8,128)} %param.27) | copy-start | bytes 2752516
  7.2 18.8 %copy-start.78 = (s32[14,8]{0,1:T(8,128)S(1)}, s32[14,8]{0,1:T(8,128)}, u32[]{:S(2)}) copy-start(s32[14,8]{0,1:T(8,128)} %param.26) | copy-start | bytes 1348
  7.2 19.4 %copy-start.130 = (f32[8,1024]{1,0:T(8,128)S(1)}, f32[8,1024]{1,0:T(8,128)}, u32[]{:S(2)}) copy-start(f32[8,1024]{1,0:T(8,128)} %param.22) | copy-start | bytes 98308
  7.2 19.4 %copy-start.131 = (s32[2]{0:T(128)S(1)}, s32[2]{0:T(128)}, u32[]{:S(2)}) copy-start(s32[2]{0:T(128)} %param.21) | copy-start | bytes 28
  7.2 66.9 %all-gather.11.cloned.1.call-start = ((), (), s32[]{:S(2)}) async-start(), calls=%async_computation.9 | async-start | bytes 3538944 | tf_op jit(solution)/shard_map/all_gather | solution.py:209
  10.7 137.6 %all-gather.15.cloned.1.call-start = ((), (), s32[]{:S(2)}) async-start(), calls=%async_computation.11 | async-start | bytes 4718592 | tf_op jit(solution)/shard_map/all_gather | solution.py:50
  12.7 158.9 %all-gather.13.cloned.1.call-start = ((), (), s32[]{:S(2)}) async-start(), calls=%async_computation.10 | async-start | bytes 2621440 | tf_op jit(solution)/shard_map/all_gather | solution.py:103
  26.7 67.5 %copy-start.95 = (f32[1024]{0:T(1024)}, f32[1024]{0:T(1024)S(1)}, u32[]{:S(2)}) copy-start(f32[1024]{0:T(1024)S(1)} %get-tuple-element.293) | copy-start | bytes 12292
  26.7 67.5 %copy-start.97 = (f32[1024]{0:T(1024)}, f32[1024]{0:T(1024)S(1)}, u32[]{:S(2)}) copy-start(f32[1024]{0:T(1024)S(1)} %get-tuple-element.294) | copy-start | bytes 12292
  26.7 67.5 %copy-start.101 = (f32[1024]{0:T(1024)}, f32[1024]{0:T(1024)S(1)}, u32[]{:S(2)}) copy-start(f32[1024]{0:T(1024)S(1)} %get-tuple-element.224) | copy-start | bytes 12292
  26.7 67.5 %copy-start.103 = (f32[1024]{0:T(1024)}, f32[1024]{0:T(1024)S(1)}, u32[]{:S(2)}) copy-start(f32[1024]{0:T(1024)S(1)} %get-tuple-element.225) | copy-start | bytes 12292
  26.9 66.6 %copy-start.109 = (bf16[2,1024]{1,0:T(2,128)(2,1)}, bf16[2,1024]{1,0:T(2,128)(2,1)S(1)}, u32[]{:S(2)}) copy-start(bf16[2,1024]{1,0:T(2,128)(2,1)S(1)} %fusion.150) | copy-start | bytes 12292
  94.1 58.1 %copy-start.105 = (f32[1,1,256]{2,0,1:T(1,128)}, f32[1,1,256]{2,0,1:T(1,128)S(1)}, u32[]{:S(2)}) copy-start(f32[1,1,256]{2,0,1:T(1,128)S(1)} %get-tuple-element.218) | copy-start | bytes 3076
  94.1 58.1 %copy-start.107 = (f32[1,1,256]{2,0,1:T(1,128)}, f32[1,1,256]{2,0,1:T(1,128)S(1)}, u32[]{:S(2)}) copy-start(f32[1,1,256]{2,0,1:T(1,128)S(1)} %get-tuple-element.213) | copy-start | bytes 3076
  95.8 100.6 %all-gather.19.cloned.1.call-start = ((), (), s32[]{:S(2)}) async-start(), calls=%async_computation.15 | async-start | bytes 2621440 | tf_op jit(solution)/shard_map/all_gather | solution.py:103
  97.8 180.9 %reduce-scatter.14.cloned.1.call-start = ((), (), s32[]{:S(2)}) async-start(), calls=%async_computation.16 | async-start | bytes 2621440 | tf_op jit(solution)/shard_map/reduce_scatter | solution.py:61
  99.7 114.0 %copy-start.71 = (f32[1024,32]{0,1:T(8,128)}, f32[1024,32]{0,1:T(8,128)S(1)}, u32[]{:S(2)}) copy-start(f32[1024,32]{0,1:T(8,128)S(1)} %get-tuple-element.234) | copy-start | bytes 393220
  175.4 21.0 %copy-start.80 = (bf16[1024,1,256]{0,2,1:T(8,128)(2,1)S(1)}, bf16[1024,1,256]{0,2,1:T(8,128)(2,1)}, u32[]{:S(2)}) copy-start(bf16[1024,1,256]{0,2,1:T(8,128)(2,1)} %copy.67) | copy-start | bytes 1572868
  175.5 92.6 %copy-start.21 = (bf16[1024,1,256]{0,2,1:T(8,128)(2,1)}, bf16[1024,1,256]{0,2,1:T(8,128)(2,1)S(1)}, u32[]{:S(2)}) copy-start(bf16[1024,1,256]{0,2,1:T(8,128)(2,1)S(1)} %slice.800) | copy-start | bytes 1572868
  247.2 66.1 %reduce-scatter.10.cloned.1.call-start = ((), (), s32[]{:S(2)}) async-start(), calls=%async_computation.12 | async-start | bytes 2621440 | tf_op jit(solution)/shard_map/reduce_scatter | solution.py:61
  273.1 79.7 %all-gather.21.cloned.1.call-start = ((), (), s32[]{:S(2)}) async-start(), calls=%async_computation.17 | async-start | bytes 2621440 | tf_op jit(solution)/shard_map/all_gather | solution.py:103
  328.8 49.0 %all-gather.27.cloned.1.call-start = ((), (), s32[]{:S(2)}) async-start(), calls=%async_computation.23 | async-start | bytes 2621440 | tf_op jit(solution)/shard_map/all_gather | solution.py:67
  328.9 10.8 %copy-start.46 = (bf16[8,128,256]{2,1,0:T(8,128)(2,1)S(1)}, bf16[8,128,256]{2,1,0:T(8,128)(2,1)}, u32[]{:S(2)}) copy-start(bf16[8,128,256]{2,1,0:T(8,128)(2,1)} %get-tuple-element.142) | copy-start | bytes 1572868
  332.0 70.8 %all-gather.17.cloned.1.call-start = ((), (), s32[]{:S(2)}) async-start(), calls=%async_computation.13 | async-start | bytes 2621440 | tf_op jit(solution)/shard_map/all_gather | solution.py:103
  332.8 94.3 %all-gather.23.cloned.1.call-start = ((), (), s32[]{:S(2)}) async-start(), calls=%async_computation.19 | async-start | bytes 2621440 | tf_op jit(solution)/shard_map/all_gather | solution.py:67
  333.4 127.8 %reduce-scatter.22.cloned.1.call-start = ((), (), s32[]{:S(2)}) async-start(), calls=%async_computation.24 | async-start | bytes 2621440 | tf_op jit(solution)/shard_map/reduce_scatter | solution.py:107
  344.3 92.1 %copy-start.81 = (bf16[8,128,256]{2,1,0:T(8,128)(2,1)}, bf16[8,128,256]{2,1,0:T(8,128)(2,1)S(1)}, u32[]{:S(2)}) copy-start(bf16[8,128,256]{2,1,0:T(8,128)(2,1)S(1)} %broadcast_select_fusion) | copy-start | bytes 1572868
  352.8 25.0 %copy-start.82 = (bf16[8,128,256]{2,1,0:T(8,128)(2,1)S(1)}, bf16[8,128,256]{2,1,0:T(8,128)(2,1)}, u32[]{:S(2)}) copy-start(bf16[8,128,256]{2,1,0:T(8,128)(2,1)} %broadcast_select_fusion.1) | copy-start | bytes 1572868
  386.8 108.3 %reduce-scatter.18.cloned.1.call-start = ((), (), s32[]{:S(2)}) async-start(), calls=%async_computation.20 | async-start | bytes 2621440 | tf_op jit(solution)/shard_map/reduce_scatter | solution.py:107
  436.1 93.0 %reduce-scatter.16.cloned.1.call-start = ((), (), s32[]{:S(2)}) async-start(), calls=%async_computation.18 | async-start | bytes 2621440 | tf_op jit(solution)/shard_map/reduce_scatter | solution.py:61
  441.1 54.0 %copy-start.9 = (bf16[1024,256]{1,0:T(8,128)(2,1)S(1)}, bf16[1024,256]{1,0:T(8,128)(2,1)}, u32[]{:S(2)}) copy-start(bf16[1024,256]{1,0:T(8,128)(2,1)} %reduce-scatter.14.cloned.1.call-done) | copy-start | bytes 1572868
  441.1 54.0 %copy-start.10 = (bf16[1024,256]{1,0:T(8,128)(2,1)S(1)}, bf16[1024,256]{1,0:T(8,128)(2,1)}, u32[]{:S(2)}) copy-start(bf16[1024,256]{1,0:T(8,128)(2,1)} %reduce-scatter.10.cloned.1.call-done) | copy-start | bytes 1572868
  441.1 122.0 %reduce-scatter.12.cloned.1.call-start = ((), (), s32[]{:S(2)}) async-start(), calls=%async_computation.14 | async-start | bytes 2621440 | tf_op jit(solution)/shard_map/reduce_scatter | solution.py:61
  446.0 144.4 %all-gather.29.cloned.1.call-start = ((), (), s32[]{:S(2)}) async-start(), calls=%async_computation.25 | async-start | bytes 2621440 | tf_op jit(solution)/shard_map/all_gather | solution.py:67
  453.8 113.7 %copy-start.132 = (s32[8]{0:T(128)}, s32[8]{0:T(128)S(1)}, u32[]{:S(2)}) copy-start(s32[8]{0:T(128)S(1)} %get-tuple-element.38) | copy-start | bytes 100
  457.6 40.4 %copy-start.140 = (s32[8]{0:T(128)}, s32[8]{0:T(128)S(1)}, u32[]{:S(2)}) copy-start(s32[8]{0:T(128)S(1)} %get-tuple-element.34) | copy-start | bytes 100
  567.4 64.6 %all-gather.25.cloned.1.call-start = ((), (), s32[]{:S(2)}) async-start(), calls=%async_computation.21 | async-start | bytes 2621440 | tf_op jit(solution)/shard_map/all_gather | solution.py:67
  573.7 19.8 %copy-start.24 = (bf16[1024,1,256]{0,2,1:T(8,128)(2,1)S(1)}, bf16[1024,1,256]{0,2,1:T(8,128)(2,1)}, u32[]{:S(2)}) copy-start(bf16[1024,1,256]{0,2,1:T(8,128)(2,1)} %slice.799) | copy-start | bytes 1572868
  573.7 223.9 %reduce-scatter.24.cloned.1.call-start = ((), (), s32[]{:S(2)}) async-start(), calls=%async_computation.26 | async-start | bytes 2621440 | tf_op jit(solution)/shard_map/reduce_scatter | solution.py:107
  598.1 14.9 %slice-start.4 = ((s8[8388608]{0:T(1024)(128)(4,1)}), s8[4194304]{0:T(1024)(128)(4,1)S(1)}, s32[]{:S(2)}) async-start(s8[8388608]{0:T(1024)(128)(4,1)} %bitcast.345), calls=%async_computation.32 | async-start | bytes 8388608
  598.1 14.9 %slice-start.6 = ((s8[8388608]{0:T(1024)(128)(4,1)}), s8[4194304]{0:T(1024)(128)(4,1)S(1)}, s32[]{:S(2)}) async-start(s8[8388608]{0:T(1024)(128)(4,1)} %bitcast.347), calls=%async_computation.34 | async-start | bytes 8388608
  598.1 15.6 %slice-start.5 = ((s8[8388608]{0:T(1024)(128)(4,1)}), s8[4194304]{0:T(1024)(128)(4,1)S(1)}, s32[]{:S(2)}) async-start(s8[8388608]{0:T(1024)(128)(4,1)} %bitcast.345), calls=%async_computation.33 | async-start | bytes 8388608
  598.1 17.1 %slice-start.7 = ((s8[8388608]{0:T(1024)(128)(4,1)}), s8[4194304]{0:T(1024)(128)(4,1)S(1)}, s32[]{:S(2)}) async-start(s8[8388608]{0:T(1024)(128)(4,1)} %bitcast.347), calls=%async_computation.35 | async-start | bytes 8388608
  639.7 14.1 %slice-start = ((s8[8388608]{0:T(1024)(128)(4,1)}), s8[4194304]{0:T(1024)(128)(4,1)S(1)}, s32[]{:S(2)}) async-start(s8[8388608]{0:T(1024)(128)(4,1)} %bitcast.341), calls=%async_computation.28 | async-start | bytes 8388608
  639.7 14.1 %slice-start.2 = ((s8[8388608]{0:T(1024)(128)(4,1)}), s8[4194304]{0:T(1024)(128)(4,1)S(1)}, s32[]{:S(2)}) async-start(s8[8388608]{0:T(1024)(128)(4,1)} %bitcast.343), calls=%async_computation.30 | async-start | bytes 8388608
  639.7 15.2 %slice-start.1 = ((s8[8388608]{0:T(1024)(128)(4,1)}), s8[4194304]{0:T(1024)(128)(4,1)S(1)}, s32[]{:S(2)}) async-start(s8[8388608]{0:T(1024)(128)(4,1)} %bitcast.341), calls=%async_computation.29 | async-start | bytes 8388608
  639.8 16.4 %slice-start.3 = ((s8[8388608]{0:T(1024)(128)(4,1)}), s8[4194304]{0:T(1024)(128)(4,1)S(1)}, s32[]{:S(2)}) async-start(s8[8388608]{0:T(1024)(128)(4,1)} %bitcast.343), calls=%async_computation.31 | async-start | bytes 8388608
  733.9 65.8 %reduce-scatter.20.cloned.1.call-start = ((), (), s32[]{:S(2)}) async-start(), calls=%async_computation.22 | async-start | bytes 2621440 | tf_op jit(solution)/shard_map/reduce_scatter | solution.py:107
  766.7 275.1 %reduce-scatter.26.cloned.1.call-start = ((), (), s32[]{:S(2)}) async-start(), calls=%async_computation.27 | async-start | bytes 8257536 | tf_op jit(solution)/shard_map/reduce_scatter | solution.py:55
  788.6 11.0 %copy-start.96 = (f32[1024]{0:T(1024)S(1)}, f32[1024]{0:T(1024)}, u32[]{:S(2)}) copy-start(f32[1024]{0:T(1024)} %copy-done.95) | copy-start | bytes 12292
  788.7 11.0 %copy-start.98 = (f32[1024]{0:T(1024)S(1)}, f32[1024]{0:T(1024)}, u32[]{:S(2)}) copy-start(f32[1024]{0:T(1024)} %copy-done.97) | copy-start | bytes 12292
  788.7 11.0 %copy-start.102 = (f32[1024]{0:T(1024)S(1)}, f32[1024]{0:T(1024)}, u32[]{:S(2)}) copy-start(f32[1024]{0:T(1024)} %copy-done.101) | copy-start | bytes 12292
  788.7 11.0 %copy-start.104 = (f32[1024]{0:T(1024)S(1)}, f32[1024]{0:T(1024)}, u32[]{:S(2)}) copy-start(f32[1024]{0:T(1024)} %copy-done.103) | copy-start | bytes 12292
  788.7 11.0 %copy-start.106 = (f32[1,1,256]{2,0,1:T(1,128)S(1)}, f32[1,1,256]{2,0,1:T(1,128)}, u32[]{:S(2)}) copy-start(f32[1,1,256]{2,0,1:T(1,128)} %copy-done.105) | copy-start | bytes 3076
  788.7 11.0 %copy-start.108 = (f32[1,1,256]{2,0,1:T(1,128)S(1)}, f32[1,1,256]{2,0,1:T(1,128)}, u32[]{:S(2)}) copy-start(f32[1,1,256]{2,0,1:T(1,128)} %copy-done.107) | copy-start | bytes 3076
  788.7 23.7 %copy-start.11 = (bf16[1024,256]{1,0:T(8,128)(2,1)S(1)}, bf16[1024,256]{1,0:T(8,128)(2,1)}, u32[]{:S(2)}) copy-start(bf16[1024,256]{1,0:T(8,128)(2,1)} %reduce-scatter.10.cloned.1.call-done) | copy-start | bytes 1572868
  802.2 13.5 %copy-start.110 = (bf16[2,1024]{1,0:T(2,128)(2,1)S(1)}, bf16[2,1024]{1,0:T(2,128)(2,1)}, u32[]{:S(2)}) copy-start(bf16[2,1024]{1,0:T(2,128)(2,1)} %copy-done.109) | copy-start | bytes 12292
  862.0 13.6 %copy-start.122 = (pred[8]{0:T(512)(128)(4,1)S(1)}, pred[8]{0:T(512)(128)(4,1)}, u32[]{:S(2)}) copy-start(pred[8]{0:T(512)(128)(4,1)} %compare_and_fusion.8) | copy-start | bytes 28
  866.6 13.5 %copy-start.120 = (pred[8]{0:T(512)(128)(4,1)S(1)}, pred[8]{0:T(512)(128)(4,1)}, u32[]{:S(2)}) copy-start(pred[8]{0:T(512)(128)(4,1)} %compare_and_fusion.9) | copy-start | bytes 28
  871.1 13.4 %copy-start.121 = (pred[8]{0:T(512)(128)(4,1)S(1)}, pred[8]{0:T(512)(128)(4,1)}, u32[]{:S(2)}) copy-start(pred[8]{0:T(512)(128)(4,1)} %compare_and_fusion.10) | copy-start | bytes 28
  907.3 43.8 %copy-start.100 = (f32[13,256]{1,0:T(8,128)S(1)}, f32[13,256]{1,0:T(8,128)}, u32[]{:S(2)}) copy-start(f32[13,256]{1,0:T(8,128)} %param.29) | copy-start | bytes 39940
  907.4 43.8 %copy-start.111 = (f32[13,256]{1,0:T(8,128)S(1)}, f32[13,256]{1,0:T(8,128)}, u32[]{:S(2)}) copy-start(f32[13,256]{1,0:T(8,128)} %param.31) | copy-start | bytes 39940
  907.4 43.8 %copy-start.112 = (f32[13,256]{1,0:T(8,128)S(1)}, f32[13,256]{1,0:T(8,128)}, u32[]{:S(2)}) copy-start(f32[13,256]{1,0:T(8,128)} %param.30) | copy-start | bytes 39940
  953.8 90.3 %copy-start.64 = (f32[128,14,256]{2,0,1:T(8,128)S(1)}, f32[128,14,256]{2,0,1:T(8,128)}, u32[]{:S(2)}) copy-start(f32[128,14,256]{2,0,1:T(8,128)} %param.25) | copy-start | bytes 5505028
  (113 other events, 477.4 us)
Sparse Core Ops, SparseCore 0:
  10.9 63.1 all-gather.10
  76.3 71.9 all-gather.14
  150.5 21.1 all-gather.12
  173.6 22.8 all-gather.18
  247.4 31.3 reduce-scatter.13
  281.9 31.4 reduce-scatter.9
  329.0 23.8 all-gather.20
  354.9 22.8 all-gather.26
  379.9 22.8 all-gather.16
  404.2 22.8 all-gather.22
  429.6 31.4 reduce-scatter.21
  463.7 31.4 reduce-scatter.17
  497.7 31.4 reduce-scatter.15
  531.7 31.3 reduce-scatter.11
  567.5 22.8 all-gather.28
  592.4 22.8 all-gather.24
  734.0 31.5 reduce-scatter.23
  768.2 31.4 reduce-scatter.19
  907.4 134.4 reduce-scatter.25
where the time goes:
time: 1070 us; the launch traced here: 1060 us
  waiting for transfers between devices  413 us (39%)
  matrix products  199 us (19%)
  other arithmetic  186 us (17%)
  local copies, waits for them, and re-layouts  166 us (16%)
  blocking collectives  82.8 us (8%)
  between operations  16.3 us (2%)
    reduce_scatter x4, waiting for transfers between devices, branch_total(): lax.psum_scatter(partial_rows.astype(jnp.bfloat16), 'mp', scatter_dimensi...  93.6 us
    reduce_scatter x1, waiting for transfers between devices, reduce_grads(): lax.psum_scatter(values.astype(jnp.bfloat16), 'dp', scatter_dimension=0,...  85.2 us
    all_gather x4, waiting for transfers between devices, branch_spread(): return lax.all_gather(grad_rows, 'mp', axis=1, tiled=True)  56.9 us
    all_gather x1, waiting for transfers between devices, gather_block(): whole_rows = lax.all_gather(low_weights[:, :8, :], 'dp', axis=0, tiled=True)  48.6 us
    all_gather x1, waiting for transfers between devices, body(): mod_whole = lax.all_gather(low_weights[:, 8:, :], 'dp', axis=0, tiled=True)  47.2 us
    another operation x16, other arithmetic  44.2 us
    all_gather x4, waiting for transfers between devices, modulated(): return (lax.all_gather(low_rows, 'mp', axis=1, tiled=True), normed, inverse)  43.6 us
    psum x1, blocking collectives, body(): bias_grad = lax.psum(bias_local, 'dp')  39.7 us
  transfers between devices with their start and end apart: 19, of which 17 were waited for; matrix products, arithmetic and copies ran while one was open for 25% of the time, Pallas kernels for 0%

commit v1 on v0

--- a/solution.py
+++ b/solution.py
@@ -359,7 +359,11 @@
         stored_order(jnp.concatenate([weight_total, grad_mod_weight], axis=1), owners)
     )
     bias_local = jnp.concatenate([bias_total, jnp.sum(grad_mods, axis=0)], axis=0)
-    bias_grad = lax.psum(bias_local, "dp")
+    bias_grad = bias_local
+    for hop in (1, 2, 4):
+        bias_grad = bias_grad + lax.ppermute(
+            bias_grad, "dp", [(dev, dev ^ hop) for dev in range(8)]
+        )
     turned = jnp.einsum("kij,ikc->jkc", left_basis, reduced, precision=highest)
     turned = jnp.einsum("jkc,kce->jke", turned, right_basis, precision=highest)
     first_new = soap_first * first_moments + (1.0 - soap_first) * turned

time: 1070 us -> 1070 us (level)
  blocking collectives: 82.8 us -> 43.1 us
  waiting for transfers between devices: 413 us -> 451 us
    psum x1 -> x0, blocking collectives: 39.7 us -> none  [body(): bias_grad = lax.psum(bias_local, 'dp')]
    reduce_scatter x1, waiting for transfers between devices: 85.2 us -> 116 us  [reduce_grads(): lax.psum_scatter(values.astype(jnp.bfloat16), 'dp', scatter_dimension=0,...]
    unnamed x334 -> x340, local copies, waits for them, and re-layouts: 28.2 us -> 28.2 us
  transfers between devices with their start and end apart: 19 -> 22, of which waited for: 17 -> 20; matrix products, arithmetic and copies ran while one was open for 25% -> 25% of each run, Pallas kernels for 0% -> 0%
where the time goes in v1:
time: 1070 us
  waiting for transfers between devices  451 us (42%)
  matrix products  199 us (19%)
  other arithmetic  184 us (17%)
  local copies, waits for them, and re-layouts  166 us (16%)
  blocking collectives  43.1 us (4%)
  between operations  16.3 us (2%)
    reduce_scatter x1, waiting for transfers between devices, reduce_grads(): lax.psum_scatter(values.astype(jnp.bfloat16), 'dp', scatter_dimension=0,...  116 us
    reduce_scatter x4, waiting for transfers between devices, branch_total(): lax.psum_scatter(partial_rows.astype(jnp.bfloat16), 'mp', scatter_dimensi...  93.6 us
    all_gather x4, waiting for transfers between devices, branch_spread(): return lax.all_gather(grad_rows, 'mp', axis=1, tiled=True)  56.9 us
    all_gather x1, waiting for transfers between devices, gather_block(): whole_rows = lax.all_gather(low_weights[:, :8, :], 'dp', axis=0, tiled=True)  48.6 us
    all_gather x1, waiting for transfers between devices, body(): mod_whole = lax.all_gather(low_weights[:, 8:, :], 'dp', axis=0, tiled=True)  47.2 us
    another operation x16, other arithmetic  44.2 us
    all_gather x4, waiting for transfers between devices, modulated(): return (lax.all_gather(low_rows, 'mp', axis=1, tiled=True), normed, inverse)  43.6 us
    dot_general x4, matrix products, attend_back(): jnp.einsum('qhd,khd->hqk', grad_rows, values_in, preferred_element_type=j...  38 us
  transfers between devices with their start and end apart: 22, of which 20 were waited for; matrix products, arithmetic and copies ran while one was open for 25% of the time, Pallas kernels for 0%

profile of v1, /device:TPU:0, one launch (start us, length us, event | category | flops | bytes accessed | tf_op | source)
XLA Modules:
  0.0 1065.9 jit_solution(9125322918919355056)
XLA Ops:
  13.4 12.6 %all-reduce.3 = (f32[1024]{0:T(1024)S(1)}, f32[1024]{0:T(1024)S(1)}, f32[1024]{0:T(1024)S(1)}, f32[1024]{0:T(1024)S(1)}) all-reduce(f32[1024]{0:T(1024)S(1)} %get-tuple-element.61, f32[1024]{0:T(1024)S(1)} %get-tuple-element.60, f32[1024]{0:T(1024)S(1)} %get-tuple-element.62, ...), channel_id=1, replica_groups=mesh['dp'=8,'mp'=4] {'mp'}, use_global_device_ids=true, to_apply=%region_3.5 | all-reduce | flops 4096 | bytes 32768 | tf_op jit(solution)/shard_map/psum | solution.py:97
  26.9 47.2 %all-gather.11.cloned.1.call-done = bf16[1024,6,256]{2,0,1:T(8,128)(2,1)} async-done(((bf16[128,6,256]{2,0,1:T(8,128)(2,1)}), bf16[1024,6,256]{2,0,1:T(8,128)(2,1)}) %all-gather.11.cloned.1.call-update) | async-done | bytes 3145744 | tf_op jit(solution)/shard_map/all_gather | solution.py:209
  74.1 3.2 slice_bitcast_fusion.22
  99.7 48.6 %all-gather.15.cloned.1.call-done = bf16[1024,8,256]{2,0,1:T(8,128)(2,1)} async-done(((bf16[128,8,256]{2,0,1:T(8,128)(2,1)}), bf16[1024,8,256]{2,0,1:T(8,128)(2,1)}) %all-gather.15.cloned.1.call-update) | async-done | bytes 4194320 | tf_op jit(solution)/shard_map/all_gather | solution.py:50
  148.3 3.8 slice_bitcast_fusion.17
  171.6 3.8 fusion.59
  177.0 19.5 %all-gather.19.cloned.1.call-done = bf16[1024,1024]{1,0:T(8,128)(2,1)} async-done(((bf16[1024,256]{1,0:T(8,128)(2,1)}), bf16[1024,1024]{1,0:T(8,128)(2,1)}) %all-gather.19.cloned.1.call-update) | async-done | bytes 2097168 | tf_op jit(solution)/shard_map/all_gather | solution.py:103
  196.5 3.7 fusion.62
  213.7 8.6 subtract_convert_fusion.4
  225.5 3.4 fusion.131
  233.2 3.4 exponential_reduce_fusion.1
  247.3 2.9 pad_maximum_fusion.10
  251.5 3.5 fusion.132
  259.4 3.4 exponential_reduce_fusion.3
  274.8 4.0 reduce-scatter.14.cloned.1.call-done
  278.8 34.6 %reduce-scatter.10.cloned.1.call-done = bf16[1024,256]{1,0:T(8,128)(2,1)} async-done(((bf16[1024,1024]{1,0:T(8,128)(2,1)}), bf16[1024,256]{1,0:T(8,128)(2,1)}) %reduce-scatter.10.cloned.1.call-update) | async-done | bytes 524304 | tf_op jit(solution)/shard_map/reduce_scatter | solution.py:61
  315.6 10.1 all-reduce.2
  325.8 3.0 add_convert_fusion.3
  328.9 3.1 convert_reduce_fusion.10
  346.2 6.7 all-gather.21.cloned.1.call-done
  352.8 4.5 fusion.32
  357.4 20.5 %all-gather.27.cloned.1.call-done = bf16[1024,1024]{1,0:T(8,128)(2,1)} async-done(((bf16[1024,256]{1,0:T(8,128)(2,1)}), bf16[1024,1024]{1,0:T(8,128)(2,1)}) %all-gather.27.cloned.1.call-update) | async-done | bytes 2097168 | tf_op jit(solution)/shard_map/all_gather | solution.py:67
  377.8 5.4 convert_reduce_fusion.2
  386.9 16.0 %all-gather.17.cloned.1.call-done = bf16[1024,1024]{1,0:T(8,128)(2,1)} async-done(((bf16[1024,256]{1,0:T(8,128)(2,1)}), bf16[1024,1024]{1,0:T(8,128)(2,1)}) %all-gather.17.cloned.1.call-update) | async-done | bytes 2097168 | tf_op jit(solution)/shard_map/all_gather | solution.py:103
  402.8 4.4 fusion.40
  407.2 19.9 %all-gather.23.cloned.1.call-done = bf16[1024,1024]{1,0:T(8,128)(2,1)} async-done(((bf16[1024,256]{1,0:T(8,128)(2,1)}), bf16[1024,1024]{1,0:T(8,128)(2,1)}) %all-gather.23.cloned.1.call-update) | async-done | bytes 2097168 | tf_op jit(solution)/shard_map/all_gather | solution.py:67
  427.1 5.4 convert_reduce_fusion.3
  436.4 4.7 bitcast_convert_fusion.4
  441.2 4.8 bitcast_convert_fusion.5
  461.2 34.0 %reduce-scatter.18.cloned.1.call-done = bf16[1024,256]{1,0:T(8,128)(2,1)} async-done(((bf16[1024,1024]{1,0:T(8,128)(2,1)}), bf16[1024,256]{1,0:T(8,128)(2,1)}) %reduce-scatter.18.cloned.1.call-update) | async-done | bytes 524304 | tf_op jit(solution)/shard_map/reduce_scatter | solution.py:107
  498.0 10.1 all-reduce.1
  508.2 21.0 %reduce-scatter.16.cloned.1.call-done = bf16[1024,256]{1,0:T(8,128)(2,1)} async-done(((bf16[1024,1024]{1,0:T(8,128)(2,1)}), bf16[1024,256]{1,0:T(8,128)(2,1)}) %reduce-scatter.16.cloned.1.call-update) | async-done | bytes 524304 | tf_op jit(solution)/shard_map/reduce_scatter | solution.py:61
  529.2 34.0 %reduce-scatter.12.cloned.1.call-done = bf16[1024,256]{1,0:T(8,128)(2,1)} async-done(((bf16[1024,1024]{1,0:T(8,128)(2,1)}), bf16[1024,256]{1,0:T(8,128)(2,1)}) %reduce-scatter.12.cloned.1.call-update) | async-done | bytes 524304 | tf_op jit(solution)/shard_map/reduce_scatter | solution.py:61
  563.2 4.2 convert_reduce_fusion.11
  569.8 3.9 convert_reduce_fusion.13
  573.8 16.6 %all-gather.29.cloned.1.call-done = bf16[1024,1024]{1,0:T(8,128)(2,1)} async-done(((bf16[1024,256]{1,0:T(8,128)(2,1)}), bf16[1024,1024]{1,0:T(8,128)(2,1)}) %all-gather.29.cloned.1.call-update) | async-done | bytes 2097168 | tf_op jit(solution)/shard_map/all_gather | solution.py:67
  593.6 4.5 fusion.200
  598.1 14.9 %multiply_reduce_fusion = (f32[4,512]{1,0:T(4,128)S(1)}, f32[4,512]{1,0:T(4,128)S(1)}, f32[4,512,1024]{2,1,0:T(8,128)}) fusion(f32[4,512,1024]{2,1,0:T(8,128)} %copy-done.3, f32[4,512]{1,0:T(4,128)S(1)} %log_add_fusion, pred[1024]{0:T(1024)(128)(4,1)S(1)} %iota_compare_fusion, f32[4,512,1024]{2,1,0:T(8,128)} %fusion.200, f32[4,512]{1,0:T(4,128)S(1)} %log_add_fusion.1, ...), kind=kOutput, calls=%fused_computation.31 | convolution fusion | flops 289402880 | bytes 34374656 | tf_op jit(solution)/shard_map/qhd,khd->hqk/dot_general | solution.py:165
  615.2 9.9 multiply_convert_fusion
  635.2 4.5 fusion.198
  639.8 14.1 %multiply_reduce_fusion.2 = (f32[4,512]{1,0:T(4,128)S(1)}, f32[4,512]{1,0:T(4,128)S(1)}, f32[4,512,1024]{2,1,0:T(8,128)}) fusion(f32[4,512,1024]{2,1,0:T(8,128)} %copy-done.2, f32[4,512]{1,0:T(4,128)S(1)} %log_add_fusion.2, pred[1024]{0:T(1024)(128)(4,1)S(1)} %iota_compare_fusion.1, f32[4,512,1024]{2,1,0:T(8,128)} %fusion.198, ...), kind=kOutput, calls=%fused_computation.35 | convolution fusion | flops 289402880 | bytes 34374656 | tf_op jit(solution)/shard_map/qhd,khd->hqk/dot_general | solution.py:165
  656.1 10.3 multiply_convert_fusion.2
  670.5 6.1 fusion.88
  678.7 4.5 fusion.92
  693.1 4.5 fusion.90
  707.3 8.5 subtract_convert_fusion.3
  721.8 3.1 pad_maximum_fusion.17
  729.0 4.9 bitcast_convert_fusion
  734.2 5.4 fusion.142
  739.6 6.6 fusion.87
  748.3 3.1 pad_maximum_fusion.14
  755.4 2.9 pad_maximum_fusion.15
  761.7 5.0 bitcast_convert_fusion.2
  767.0 4.6 fusion.30
  788.7 8.9 maximum_add_fusion
  802.3 10.1 all-reduce
  812.4 3.2 multiply_reduce_fusion.5
  815.7 4.2 fusion.146
  820.0 6.7 pad_maximum_fusion
  826.7 5.7 slice_bitcast_fusion
  923.3 2.9 collective-permute-done.2
  926.9 116.1 %reduce-scatter.26.cloned.1.call-done = bf16[128,14,256]{2,0,1:T(8,128)(2,1)} async-done(((bf16[1024,14,256]{2,0,1:T(8,128)(2,1)}), bf16[128,14,256]{2,0,1:T(8,128)(2,1)}) %reduce-scatter.26.cloned.1.call-update) | async-done | bytes 917520 | tf_op jit(solution)/shard_map/reduce_scatter | solution.py:55
  1045.3 4.3 fusion.46
  1052.4 5.4 fusion.197
  (657 shorter events, 326.0 us)
Async XLA Ops:
  7.2 1035.8 %copy-start = (f32[14,128,128]{2,1,0:T(8,128)S(1)}, f32[14,128,128]{2,1,0:T(8,128)}, u32[]{:S(2)}) copy-start(f32[14,128,128]{2,1,0:T(8,128)} %param.27) | copy-start | bytes 2752516
  7.2 18.8 %copy-start.81 = (s32[14,8]{0,1:T(8,128)S(1)}, s32[14,8]{0,1:T(8,128)}, u32[]{:S(2)}) copy-start(s32[14,8]{0,1:T(8,128)} %param.26) | copy-start | bytes 1348
  7.2 19.4 %copy-start.133 = (f32[8,1024]{1,0:T(8,128)S(1)}, f32[8,1024]{1,0:T(8,128)}, u32[]{:S(2)}) copy-start(f32[8,1024]{1,0:T(8,128)} %param.22) | copy-start | bytes 98308
  7.2 19.4 %copy-start.134 = (s32[2]{0:T(128)S(1)}, s32[2]{0:T(128)}, u32[]{:S(2)}) copy-start(s32[2]{0:T(128)} %param.21) | copy-start | bytes 28
  7.2 66.9 %all-gather.11.cloned.1.call-start = ((), (), s32[]{:S(2)}) async-start(), calls=%async_computation.9 | async-start | bytes 3538944 | tf_op jit(solution)/shard_map/all_gather | solution.py:209
  10.7 137.6 %all-gather.15.cloned.1.call-start = ((), (), s32[]{:S(2)}) async-start(), calls=%async_computation.11 | async-start | bytes 4718592 | tf_op jit(solution)/shard_map/all_gather | solution.py:50
  12.7 158.9 %all-gather.13.cloned.1.call-start = ((), (), s32[]{:S(2)}) async-start(), calls=%async_computation.10 | async-start | bytes 2621440 | tf_op jit(solution)/shard_map/all_gather | solution.py:103
  26.7 67.5 %copy-start.98 = (f32[1024]{0:T(1024)}, f32[1024]{0:T(1024)S(1)}, u32[]{:S(2)}) copy-start(f32[1024]{0:T(1024)S(1)} %get-tuple-element.293) | copy-start | bytes 12292
  26.7 67.5 %copy-start.100 = (f32[1024]{0:T(1024)}, f32[1024]{0:T(1024)S(1)}, u32[]{:S(2)}) copy-start(f32[1024]{0:T(1024)S(1)} %get-tuple-element.294) | copy-start | bytes 12292
  26.7 67.5 %copy-start.104 = (f32[1024]{0:T(1024)}, f32[1024]{0:T(1024)S(1)}, u32[]{:S(2)}) copy-start(f32[1024]{0:T(1024)S(1)} %get-tuple-element.224) | copy-start | bytes 12292
  26.7 67.5 %copy-start.106 = (f32[1024]{0:T(1024)}, f32[1024]{0:T(1024)S(1)}, u32[]{:S(2)}) copy-start(f32[1024]{0:T(1024)S(1)} %get-tuple-element.225) | copy-start | bytes 12292
  26.9 66.6 %copy-start.112 = (bf16[2,1024]{1,0:T(2,128)(2,1)}, bf16[2,1024]{1,0:T(2,128)(2,1)S(1)}, u32[]{:S(2)}) copy-start(bf16[2,1024]{1,0:T(2,128)(2,1)S(1)} %fusion.150) | copy-start | bytes 12292
  94.1 58.1 %copy-start.108 = (f32[1,1,256]{2,0,1:T(1,128)}, f32[1,1,256]{2,0,1:T(1,128)S(1)}, u32[]{:S(2)}) copy-start(f32[1,1,256]{2,0,1:T(1,128)S(1)} %get-tuple-element.218) | copy-start | bytes 3076
  94.1 58.1 %copy-start.110 = (f32[1,1,256]{2,0,1:T(1,128)}, f32[1,1,256]{2,0,1:T(1,128)S(1)}, u32[]{:S(2)}) copy-start(f32[1,1,256]{2,0,1:T(1,128)S(1)} %get-tuple-element.213) | copy-start | bytes 3076
  95.8 100.6 %all-gather.19.cloned.1.call-start = ((), (), s32[]{:S(2)}) async-start(), calls=%async_computation.15 | async-start | bytes 2621440 | tf_op jit(solution)/shard_map/all_gather | solution.py:103
  97.8 180.9 %reduce-scatter.14.cloned.1.call-start = ((), (), s32[]{:S(2)}) async-start(), calls=%async_computation.16 | async-start | bytes 2621440 | tf_op jit(solution)/shard_map/reduce_scatter | solution.py:61
  99.7 114.0 %copy-start.74 = (f32[1024,32]{0,1:T(8,128)}, f32[1024,32]{0,1:T(8,128)S(1)}, u32[]{:S(2)}) copy-start(f32[1024,32]{0,1:T(8,128)S(1)} %get-tuple-element.234) | copy-start | bytes 393220
  175.4 21.0 %copy-start.83 = (bf16[1024,1,256]{0,2,1:T(8,128)(2,1)S(1)}, bf16[1024,1,256]{0,2,1:T(8,128)(2,1)}, u32[]{:S(2)}) copy-start(bf16[1024,1,256]{0,2,1:T(8,128)(2,1)} %copy.67) | copy-start | bytes 1572868
  175.5 92.6 %copy-start.22 = (bf16[1024,1,256]{0,2,1:T(8,128)(2,1)}, bf16[1024,1,256]{0,2,1:T(8,128)(2,1)S(1)}, u32[]{:S(2)}) copy-start(bf16[1024,1,256]{0,2,1:T(8,128)(2,1)S(1)} %slice.800) | copy-start | bytes 1572868
  247.2 66.1 %reduce-scatter.10.cloned.1.call-start = ((), (), s32[]{:S(2)}) async-start(), calls=%async_computation.12 | async-start | bytes 2621440 | tf_op jit(solution)/shard_map/reduce_scatter | solution.py:61
  273.1 79.7 %all-gather.21.cloned.1.call-start = ((), (), s32[]{:S(2)}) async-start(), calls=%async_computation.17 | async-start | bytes 2621440 | tf_op jit(solution)/shard_map/all_gather | solution.py:103
  328.8 49.0 %all-gather.27.cloned.1.call-start = ((), (), s32[]{:S(2)}) async-start(), calls=%async_computation.23 | async-start | bytes 2621440 | tf_op jit(solution)/shard_map/all_gather | solution.py:67
  332.0 70.8 %all-gather.17.cloned.1.call-start = ((), (), s32[]{:S(2)}) async-start(), calls=%async_computation.13 | async-start | bytes 2621440 | tf_op jit(solution)/shard_map/all_gather | solution.py:103
  332.8 94.4 %all-gather.23.cloned.1.call-start = ((), (), s32[]{:S(2)}) async-start(), calls=%async_computation.19 | async-start | bytes 2621440 | tf_op jit(solution)/shard_map/all_gather | solution.py:67
  333.4 127.8 %reduce-scatter.22.cloned.1.call-start = ((), (), s32[]{:S(2)}) async-start(), calls=%async_computation.24 | async-start | bytes 2621440 | tf_op jit(solution)/shard_map/reduce_scatter | solution.py:107
  344.3 92.1 %copy-start.84 = (bf16[8,128,256]{2,1,0:T(8,128)(2,1)}, bf16[8,128,256]{2,1,0:T(8,128)(2,1)S(1)}, u32[]{:S(2)}) copy-start(bf16[8,128,256]{2,1,0:T(8,128)(2,1)S(1)} %broadcast_select_fusion) | copy-start | bytes 1572868
  352.8 25.0 %copy-start.85 = (bf16[8,128,256]{2,1,0:T(8,128)(2,1)S(1)}, bf16[8,128,256]{2,1,0:T(8,128)(2,1)}, u32[]{:S(2)}) copy-start(bf16[8,128,256]{2,1,0:T(8,128)(2,1)} %broadcast_select_fusion.1) | copy-start | bytes 1572868
  386.8 108.3 %reduce-scatter.18.cloned.1.call-start = ((), (), s32[]{:S(2)}) async-start(), calls=%async_computation.20 | async-start | bytes 2621440 | tf_op jit(solution)/shard_map/reduce_scatter | solution.py:107
  436.1 93.0 %reduce-scatter.16.cloned.1.call-start = ((), (), s32[]{:S(2)}) async-start(), calls=%async_computation.18 | async-start | bytes 2621440 | tf_op jit(solution)/shard_map/reduce_scatter | solution.py:61
  441.1 54.0 %copy-start.9 = (bf16[1024,256]{1,0:T(8,128)(2,1)S(1)}, bf16[1024,256]{1,0:T(8,128)(2,1)}, u32[]{:S(2)}) copy-start(bf16[1024,256]{1,0:T(8,128)(2,1)} %reduce-scatter.14.cloned.1.call-done) | copy-start | bytes 1572868
  441.1 54.0 %copy-start.10 = (bf16[1024,256]{1,0:T(8,128)(2,1)S(1)}, bf16[1024,256]{1,0:T(8,128)(2,1)}, u32[]{:S(2)}) copy-start(bf16[1024,256]{1,0:T(8,128)(2,1)} %reduce-scatter.10.cloned.1.call-done) | copy-start | bytes 1572868
  441.2 122.0 %reduce-scatter.12.cloned.1.call-start = ((), (), s32[]{:S(2)}) async-start(), calls=%async_computation.14 | async-start | bytes 2621440 | tf_op jit(solution)/shard_map/reduce_scatter | solution.py:61
  446.0 144.4 %all-gather.29.cloned.1.call-start = ((), (), s32[]{:S(2)}) async-start(), calls=%async_computation.25 | async-start | bytes 2621440 | tf_op jit(solution)/shard_map/all_gather | solution.py:67
  453.8 113.7 %copy-start.135 = (s32[8]{0:T(128)}, s32[8]{0:T(128)S(1)}, u32[]{:S(2)}) copy-start(s32[8]{0:T(128)S(1)} %get-tuple-element.38) | copy-start | bytes 100
  457.6 40.4 %copy-start.143 = (s32[8]{0:T(128)}, s32[8]{0:T(128)S(1)}, u32[]{:S(2)}) copy-start(s32[8]{0:T(128)S(1)} %get-tuple-element.34) | copy-start | bytes 100
  567.4 64.6 %all-gather.25.cloned.1.call-start = ((), (), s32[]{:S(2)}) async-start(), calls=%async_computation.21 | async-start | bytes 2621440 | tf_op jit(solution)/shard_map/all_gather | solution.py:67
  573.7 19.8 %copy-start.25 = (bf16[1024,1,256]{0,2,1:T(8,128)(2,1)S(1)}, bf16[1024,1,256]{0,2,1:T(8,128)(2,1)}, u32[]{:S(2)}) copy-start(bf16[1024,1,256]{0,2,1:T(8,128)(2,1)} %slice.799) | copy-start | bytes 1572868
  573.8 223.9 %reduce-scatter.24.cloned.1.call-start = ((), (), s32[]{:S(2)}) async-start(), calls=%async_computation.26 | async-start | bytes 2621440 | tf_op jit(solution)/shard_map/reduce_scatter | solution.py:107
  598.1 14.9 %slice-start.4 = ((s8[8388608]{0:T(1024)(128)(4,1)}), s8[4194304]{0:T(1024)(128)(4,1)S(1)}, s32[]{:S(2)}) async-start(s8[8388608]{0:T(1024)(128)(4,1)} %bitcast.345), calls=%async_computation.32 | async-start | bytes 8388608
  598.1 14.9 %slice-start.6 = ((s8[8388608]{0:T(1024)(128)(4,1)}), s8[4194304]{0:T(1024)(128)(4,1)S(1)}, s32[]{:S(2)}) async-start(s8[8388608]{0:T(1024)(128)(4,1)} %bitcast.347), calls=%async_computation.34 | async-start | bytes 8388608
  598.1 15.6 %slice-start.5 = ((s8[8388608]{0:T(1024)(128)(4,1)}), s8[4194304]{0:T(1024)(128)(4,1)S(1)}, s32[]{:S(2)}) async-start(s8[8388608]{0:T(1024)(128)(4,1)} %bitcast.345), calls=%async_computation.33 | async-start | bytes 8388608
  598.1 17.1 %slice-start.7 = ((s8[8388608]{0:T(1024)(128)(4,1)}), s8[4194304]{0:T(1024)(128)(4,1)S(1)}, s32[]{:S(2)}) async-start(s8[8388608]{0:T(1024)(128)(4,1)} %bitcast.347), calls=%async_computation.35 | async-start | bytes 8388608
  639.8 14.1 %slice-start = ((s8[8388608]{0:T(1024)(128)(4,1)}), s8[4194304]{0:T(1024)(128)(4,1)S(1)}, s32[]{:S(2)}) async-start(s8[8388608]{0:T(1024)(128)(4,1)} %bitcast.341), calls=%async_computation.28 | async-start | bytes 8388608
  639.8 14.1 %slice-start.2 = ((s8[8388608]{0:T(1024)(128)(4,1)}), s8[4194304]{0:T(1024)(128)(4,1)S(1)}, s32[]{:S(2)}) async-start(s8[8388608]{0:T(1024)(128)(4,1)} %bitcast.343), calls=%async_computation.30 | async-start | bytes 8388608
  639.8 15.2 %slice-start.1 = ((s8[8388608]{0:T(1024)(128)(4,1)}), s8[4194304]{0:T(1024)(128)(4,1)S(1)}, s32[]{:S(2)}) async-start(s8[8388608]{0:T(1024)(128)(4,1)} %bitcast.341), calls=%async_computation.29 | async-start | bytes 8388608
  639.8 16.4 %slice-start.3 = ((s8[8388608]{0:T(1024)(128)(4,1)}), s8[4194304]{0:T(1024)(128)(4,1)S(1)}, s32[]{:S(2)}) async-start(s8[8388608]{0:T(1024)(128)(4,1)} %bitcast.343), calls=%async_computation.31 | async-start | bytes 8388608
  733.9 65.8 %reduce-scatter.20.cloned.1.call-start = ((), (), s32[]{:S(2)}) async-start(), calls=%async_computation.22 | async-start | bytes 2621440 | tf_op jit(solution)/shard_map/reduce_scatter | solution.py:107
  766.7 276.2 %reduce-scatter.26.cloned.1.call-start = ((), (), s32[]{:S(2)}) async-start(), calls=%async_computation.27 | async-start | bytes 8257536 | tf_op jit(solution)/shard_map/reduce_scatter | solution.py:55
  788.7 11.0 %copy-start.99 = (f32[1024]{0:T(1024)S(1)}, f32[1024]{0:T(1024)}, u32[]{:S(2)}) copy-start(f32[1024]{0:T(1024)} %copy-done.98) | copy-start | bytes 12292
  788.7 11.0 %copy-start.101 = (f32[1024]{0:T(1024)S(1)}, f32[1024]{0:T(1024)}, u32[]{:S(2)}) copy-start(f32[1024]{0:T(1024)} %copy-done.100) | copy-start | bytes 12292
  788.7 11.0 %copy-start.105 = (f32[1024]{0:T(1024)S(1)}, f32[1024]{0:T(1024)}, u32[]{:S(2)}) copy-start(f32[1024]{0:T(1024)} %copy-done.104) | copy-start | bytes 12292
  788.7 11.0 %copy-start.107 = (f32[1024]{0:T(1024)S(1)}, f32[1024]{0:T(1024)}, u32[]{:S(2)}) copy-start(f32[1024]{0:T(1024)} %copy-done.106) | copy-start | bytes 12292
  788.7 11.0 %copy-start.109 = (f32[1,1,256]{2,0,1:T(1,128)S(1)}, f32[1,1,256]{2,0,1:T(1,128)}, u32[]{:S(2)}) copy-start(f32[1,1,256]{2,0,1:T(1,128)} %copy-done.108) | copy-start | bytes 3076
  788.7 11.0 %copy-start.111 = (f32[1,1,256]{2,0,1:T(1,128)S(1)}, f32[1,1,256]{2,0,1:T(1,128)}, u32[]{:S(2)}) copy-start(f32[1,1,256]{2,0,1:T(1,128)} %copy-done.110) | copy-start | bytes 3076
  788.7 23.7 %copy-start.11 = (bf16[1024,256]{1,0:T(8,128)(2,1)S(1)}, bf16[1024,256]{1,0:T(8,128)(2,1)}, u32[]{:S(2)}) copy-start(bf16[1024,256]{1,0:T(8,128)(2,1)} %reduce-scatter.10.cloned.1.call-done) | copy-start | bytes 1572868
  802.3 13.5 %copy-start.113 = (bf16[2,1024]{1,0:T(2,128)(2,1)S(1)}, bf16[2,1024]{1,0:T(2,128)(2,1)}, u32[]{:S(2)}) copy-start(bf16[2,1024]{1,0:T(2,128)(2,1)} %copy-done.112) | copy-start | bytes 12292
  862.0 13.6 %copy-start.125 = (pred[8]{0:T(512)(128)(4,1)S(1)}, pred[8]{0:T(512)(128)(4,1)}, u32[]{:S(2)}) copy-start(pred[8]{0:T(512)(128)(4,1)} %compare_and_fusion.8) | copy-start | bytes 28
  866.6 13.5 %copy-start.123 = (pred[8]{0:T(512)(128)(4,1)S(1)}, pred[8]{0:T(512)(128)(4,1)}, u32[]{:S(2)}) copy-start(pred[8]{0:T(512)(128)(4,1)} %compare_and_fusion.9) | copy-start | bytes 28
  871.1 13.4 %copy-start.124 = (pred[8]{0:T(512)(128)(4,1)S(1)}, pred[8]{0:T(512)(128)(4,1)}, u32[]{:S(2)}) copy-start(pred[8]{0:T(512)(128)(4,1)} %compare_and_fusion.10) | copy-start | bytes 28
  909.8 12.1 %copy-start.28 = (f32[1024,256]{1,0:T(8,128)S(1)}, f32[1024,256]{1,0:T(8,128)}, u32[]{:S(2)}) copy-start(f32[1024,256]{1,0:T(8,128)} %get-tuple-element.181) | copy-start | bytes 3145732
  911.6 3.8 collective-permute-start
  915.4 4.6 collective-permute-start.1
  920.0 6.3 collective-permute-start.2
  921.9 123.4 %copy-start.67 = (f32[128,14,256]{2,0,1:T(8,128)S(1)}, f32[128,14,256]{2,0,1:T(8,128)}, u32[]{:S(2)}) copy-start(f32[128,14,256]{2,0,1:T(8,128)} %param.25) | copy-start | bytes 5505028
  (119 other events, 535.9 us)
Sparse Core Ops, SparseCore 0:
  10.9 63.1 all-gather.10
  76.3 71.9 all-gather.14
  150.5 21.1 all-gather.12
  173.6 22.8 all-gather.18
  247.4 31.3 reduce-scatter.13
  281.9 31.4 reduce-scatter.9
  329.0 23.8 all-gather.20
  355.0 22.8 all-gather.26
  380.0 22.8 all-gather.16
  404.2 22.8 all-gather.22
  429.6 31.4 reduce-scatter.21
  463.7 31.4 reduce-scatter.17
  497.7 31.4 reduce-scatter.15
  531.7 31.3 reduce-scatter.11
  567.5 22.8 all-gather.28
  592.4 22.8 all-gather.24
  734.1 31.5 reduce-scatter.23
  768.2 31.4 reduce-scatter.19
  907.4 135.5 reduce-scatter.25
